TPU v7x, 32 devices: a whole 2x2x4 slice. The times are simulated.
32 devices in a mesh: dp: 8 (over y, x, core), seq: 4 (over z).
Axes of the slice: x: 2, y: 2, z: 4, core: 2. Of those that a mesh axis runs over, the one named last changes fastest.
Arguments:
- hidden_in: bfloat16 [8, 2048, 1024], P('dp', 'seq'), may hold values from -6 to 6
- doc_lengths: int32 [8, 8], P('dp'), may hold values from 1 to 1024, 2048 in all within a row
- ln1_gain: float32 [1024], replicated, may hold values from 0.1 to 1.9
- ln1_bias: float32 [1024], replicated, may hold values from -1.75 to 1.75
- ln2_gain: float32 [1024], replicated, may hold values from 0.1 to 1.9
- ln2_bias: float32 [1024], replicated, may hold values from -1.75 to 1.75
- qkv_weight: bfloat16 [1024, 3072], replicated, may hold values from -0.1875 to 0.1875
- qkv_bias: float32 [3072], replicated, may hold values from -1.75 to 1.75
- dense_weight: bfloat16 [1024, 1024], replicated, may hold values from -0.75 to 0.75
- dense_bias: float32 [1024], replicated, may hold values from -1.75 to 1.75
- fc_in_weight: bfloat16 [1024, 4096], replicated, may hold values from -0.1875 to 0.1875
- fc_in_bias: float32 [4096], replicated, may hold values from -1.75 to 1.75
- fc_out_weight: bfloat16 [4096, 1024], replicated, may hold values from -0.09375 to 0.09375
- fc_out_bias: float32 [1024], replicated, may hold values from -1.75 to 1.75
- out_grad: bfloat16 [8, 2048, 1024], P('dp', 'seq'), may hold values from -8 to 8
Outputs:
- hidden_out: bfloat16 [8, 2048, 1024], P('dp', 'seq')
- grad_in: float32 [8, 2048, 1024], P('dp', 'seq')
- grad_ln1_gain: float32 [1024], P(('dp', 'seq'))
- grad_ln1_bias: float32 [1024], P(('dp', 'seq'))
- grad_ln2_gain: float32 [1024], P(('dp', 'seq'))
- grad_ln2_bias: float32 [1024], P(('dp', 'seq'))
- grad_qkv_weight: float32 [1024, 3072], P(('dp', 'seq'))
- grad_qkv_bias: float32 [3072], P(('dp', 'seq'))
- grad_dense_weight: float32 [1024, 1024], P(('dp', 'seq'))
- grad_dense_bias: float32 [1024], P(('dp', 'seq'))
- grad_fc_in_weight: float32 [1024, 4096], P(('dp', 'seq'))
- grad_fc_in_bias: float32 [4096], P(('dp', 'seq'))
- grad_fc_out_weight: float32 [4096, 1024], P(('dp', 'seq'))
- grad_fc_out_bias: float32 [1024], P(('dp', 'seq'))
Inputs may be any that keep to these rules, and one draw needn't show every extreme that they name: `doc_lengths`: each row sums to 2048; its last entry is the padding document.
All inputs are finite; a program needn't handle non-finite values.
Results may differ from a plain program's by a relative error of at most 0.0097.
Values may be sent and summed in bfloat16 or wider, within the bound.
A program may use at most 256 MiB of HBM per device.

v0:
```python
import jax
import jax.numpy as jnp
from jax import lax
from jax.sharding import PartitionSpec as P

HEADS = 16
HEAD = 64
ROT = 16
epsilon = 1e-05
masked_score = -1e30


def layout(lengths, positions):
    doc_ends = jnp.cumsum(lengths, axis=1)
    starts = doc_ends - lengths
    segment = jnp.sum((positions[None, :, None] >= doc_ends[:, None, :]).astype(jnp.int32), axis=2)
    belongs = segment[:, :, None] == jnp.arange(lengths.shape[1], dtype=jnp.int32)[None, None, :]
    doc_start = jnp.sum(jnp.where(belongs, starts[:, None, :], 0), axis=2)
    return (segment, positions[None, :] - doc_start)


def standardize(values):
    average = jnp.mean(values, axis=-1, keepdims=True)
    centered = values - average
    variance = jnp.mean(centered * centered, axis=-1, keepdims=True)
    inv_std = lax.rsqrt(variance + epsilon)
    return (centered * inv_std, inv_std)


def norm_back(d_normed, unit, inv_std, gain):
    gain_grad = jnp.sum(d_normed * unit, axis=0)
    bias_grad = jnp.sum(d_normed, axis=0)
    d_unit = d_normed * gain
    d_input = inv_std * (
        d_unit
        - jnp.mean(d_unit, axis=-1, keepdims=True)
        - unit * jnp.mean(d_unit * unit, axis=-1, keepdims=True)
    )
    return (d_input, gain_grad, bias_grad)


def rotary_tables(positions):
    half_rot = ROT // 2
    inverse = 10000.0 ** (-(2.0 * jnp.arange(half_rot, dtype=jnp.float32)) / ROT)
    angle = positions.astype(jnp.float32)[:, None] * inverse[None, :]
    return (jnp.cos(angle)[:, None, None, :], jnp.sin(angle)[:, None, None, :])


def rotate(packed, cosine, sine_part):
    half_rot = cosine.shape[-1]
    first_half = packed[..., :half_rot]
    second_half = packed[..., half_rot : 2 * half_rot]
    turned = jnp.concatenate(
        [
            first_half * cosine - second_half * sine_part,
            second_half * cosine + first_half * sine_part,
            packed[..., 2 * half_rot :],
        ],
        axis=-1,
    )
    return jnp.concatenate([turned[..., :2, :], packed[..., 2:, :]], axis=-2)


def exact_gelu(values):
    return jax.nn.gelu(values, approximate=False)


def transpose_dot(left, right):
    return lax.dot_general(
        left, right, (((0,), (0,)), ((), ())), preferred_element_type=jnp.float32
    )


def masked_scores(queries, keys_all, seg_full, first_row, last_row, score_scale):
    scores = (
        jnp.einsum(
            "bqhd,bkhd->bhqk",
            queries[:, first_row:last_row],
            keys_all[:, :last_row],
            preferred_element_type=jnp.float32,
        )
        * score_scale
    )
    query_index = jnp.arange(first_row, last_row, dtype=jnp.int32)
    key_index = jnp.arange(last_row, dtype=jnp.int32)
    allowed = (seg_full[:, first_row:last_row, None] == seg_full[:, None, :last_row]) & (
        query_index[None, :, None] >= key_index[None, None, :]
    )
    return jnp.where(allowed[:, None], scores, masked_score)


def shards(
    hidden_in,
    doc_lengths,
    ln1_gain,
    ln1_bias,
    ln2_gain,
    ln2_bias,
    qkv_weight,
    qkv_bias,
    dense_weight,
    dense_bias,
    fc_in_weight,
    fc_in_bias,
    fc_out_weight,
    fc_out_bias,
    out_grad,
):
    seqs_here, local_len, model_width = hidden_in.shape
    seq_parts = lax.axis_size("seq")
    full_len = local_len * seq_parts
    heads_here = HEADS // seq_parts
    row_count = seqs_here * local_len
    score_scale = HEAD ** (-0.5)
    block_rows = min(512, full_len)
    local_pos = lax.axis_index("seq") * local_len + jnp.arange(local_len, dtype=jnp.int32)
    seg_local, pos_local = layout(doc_lengths, local_pos)
    live_rows = (seg_local < doc_lengths.shape[1] - 1).astype(jnp.float32).reshape(row_count, 1)
    input_f32 = hidden_in.astype(jnp.float32).reshape(row_count, model_width)
    unit_attn, inv_attn = standardize(input_f32)
    unit_mlp, inv_mlp = standardize(input_f32)
    normed_attn = (unit_attn * ln1_gain + ln1_bias).astype(jnp.bfloat16)
    normed_mlp = (unit_mlp * ln2_gain + ln2_bias).astype(jnp.bfloat16)
    qkv_f32 = jnp.dot(normed_attn, qkv_weight, preferred_element_type=jnp.float32) + qkv_bias
    shaped = qkv_f32.reshape(row_count, HEADS, 3, HEAD)
    cosine, sine_part = rotary_tables(pos_local.reshape(row_count))
    turned = (
        rotate(shaped, cosine, sine_part)
        .astype(jnp.bfloat16)
        .reshape(seqs_here, local_len, 3 * model_width)
    )
    head_side = lax.all_to_all(turned, "seq", split_axis=2, concat_axis=1, tiled=True).reshape(
        seqs_here, full_len, heads_here, 3, HEAD
    )
    queries = head_side[:, :, :, 0]
    keys_all = head_side[:, :, :, 1]
    values_all = head_side[:, :, :, 2]
    seg_full, _ = layout(doc_lengths, jnp.arange(full_len, dtype=jnp.int32))
    context_parts = []
    lse_parts = []
    for first_row in range(0, full_len, block_rows):
        last_row = first_row + block_rows
        scores = masked_scores(queries, keys_all, seg_full, first_row, last_row, score_scale)
        peak_score = jnp.max(scores, axis=-1, keepdims=True)
        exponentials = jnp.exp(scores - peak_score)
        weight_sum = jnp.sum(exponentials, axis=-1, keepdims=True)
        probability = exponentials / weight_sum
        lse_parts.append(peak_score[..., 0] + jnp.log(weight_sum[..., 0]))
        context_parts.append(
            jnp.einsum(
                "bhqk,bkhd->bqhd",
                probability.astype(jnp.bfloat16),
                values_all[:, :last_row],
                preferred_element_type=jnp.float32,
            )
        )
    context_heads = (
        jnp.concatenate(context_parts, axis=1)
        .astype(jnp.bfloat16)
        .reshape(seqs_here, full_len, heads_here * HEAD)
    )
    log_sums = jnp.concatenate(lse_parts, axis=2)
    context_tok = lax.all_to_all(
        context_heads, "seq", split_axis=1, concat_axis=2, tiled=True
    ).reshape(row_count, model_width)
    attn_branch = (
        jnp.dot(context_tok, dense_weight, preferred_element_type=jnp.float32) + dense_bias
    )
    pre_act = jnp.dot(normed_mlp, fc_in_weight, preferred_element_type=jnp.float32) + fc_in_bias
    activated, gelu_pull = jax.vjp(exact_gelu, pre_act)
    act_low = activated.astype(jnp.bfloat16)
    mlp_branch = jnp.dot(act_low, fc_out_weight, preferred_element_type=jnp.float32) + fc_out_bias
    hidden_out = (
        (input_f32 + attn_branch + mlp_branch)
        .astype(jnp.bfloat16)
        .reshape(seqs_here, local_len, model_width)
    )
    gradient = out_grad.astype(jnp.float32).reshape(row_count, model_width) * live_rows
    grad_low = gradient.astype(jnp.bfloat16)
    g_dense_w = transpose_dot(context_tok, grad_low)
    g_dense_b = jnp.sum(gradient, axis=0)
    d_context = jnp.dot(grad_low, dense_weight.T, preferred_element_type=jnp.float32).astype(
        jnp.bfloat16
    )
    d_context_heads = lax.all_to_all(
        d_context.reshape(seqs_here, local_len, model_width),
        "seq",
        split_axis=2,
        concat_axis=1,
        tiled=True,
    ).reshape(seqs_here, full_len, heads_here, HEAD)
    g_out_w = transpose_dot(act_low, grad_low)
    g_out_b = jnp.sum(gradient, axis=0)
    d_act = jnp.dot(grad_low, fc_out_weight.T, preferred_element_type=jnp.float32)
    d_pre = gelu_pull(d_act)[0].astype(jnp.bfloat16)
    g_in_w = transpose_dot(normed_mlp, d_pre)
    g_in_b = jnp.sum(d_pre.astype(jnp.float32), axis=0)
    d_mlp_in = jnp.dot(d_pre, fc_in_weight.T, preferred_element_type=jnp.float32)
    d_keys = jnp.zeros((seqs_here, full_len, heads_here, HEAD), jnp.float32)
    d_values = jnp.zeros((seqs_here, full_len, heads_here, HEAD), jnp.float32)
    d_query_parts = []
    for first_row in range(0, full_len, block_rows):
        last_row = first_row + block_rows
        scores = masked_scores(queries, keys_all, seg_full, first_row, last_row, score_scale)
        probability = jnp.exp(scores - log_sums[:, :, first_row:last_row, None])
        grad_rows = d_context_heads[:, first_row:last_row]
        d_values = d_values.at[:, :last_row].add(
            jnp.einsum(
                "bhqk,bqhd->bkhd",
                probability.astype(jnp.bfloat16),
                grad_rows,
                preferred_element_type=jnp.float32,
            )
        )
        d_prob = jnp.einsum(
            "bqhd,bkhd->bhqk",
            grad_rows,
            values_all[:, :last_row],
            preferred_element_type=jnp.float32,
        )
        row_delta = jnp.sum(probability * d_prob, axis=-1, keepdims=True)
        d_scores = (probability * (d_prob - row_delta)).astype(jnp.bfloat16)
        d_query_parts.append(
            jnp.einsum(
                "bhqk,bkhd->bqhd",
                d_scores,
                keys_all[:, :last_row],
                preferred_element_type=jnp.float32,
            )
            * score_scale
        )
        d_keys = d_keys.at[:, :last_row].add(
            jnp.einsum(
                "bhqk,bqhd->bkhd",
                d_scores,
                queries[:, first_row:last_row],
                preferred_element_type=jnp.float32,
            )
            * score_scale
        )
    d_queries = jnp.concatenate(d_query_parts, axis=1)
    d_heads = (
        jnp.stack([d_queries, d_keys, d_values], axis=3)
        .astype(jnp.bfloat16)
        .reshape(seqs_here, full_len, heads_here * 3 * HEAD)
    )
    d_tokens = lax.all_to_all(d_heads, "seq", split_axis=1, concat_axis=2, tiled=True).reshape(
        row_count, HEADS, 3, HEAD
    )
    _, rotate_pull = jax.vjp(lambda packed: rotate(packed, cosine, sine_part), shaped)
    d_qkv = (
        rotate_pull(d_tokens.astype(jnp.float32))[0]
        .reshape(row_count, 3 * model_width)
        .astype(jnp.bfloat16)
    )
    g_qkv_w = transpose_dot(normed_attn, d_qkv)
    g_qkv_b = jnp.sum(d_qkv.astype(jnp.float32), axis=0)
    d_attn_in = jnp.dot(d_qkv, qkv_weight.T, preferred_element_type=jnp.float32)
    dx_attn, g_gain_one, g_bias_one = norm_back(d_attn_in, unit_attn, inv_attn, ln1_gain)
    dx_mlp, g_gain_two, g_bias_two = norm_back(d_mlp_in, unit_mlp, inv_mlp, ln2_gain)
    grad_in = (gradient + dx_attn + dx_mlp).reshape(seqs_here, local_len, model_width)
    grad_terms = (
        g_gain_one,
        g_bias_one,
        g_gain_two,
        g_bias_two,
        g_qkv_w,
        g_qkv_b,
        g_dense_w,
        g_dense_b,
        g_in_w,
        g_in_b,
        g_out_w,
        g_out_b,
    )
    reduced = (
        lax.psum_scatter(grad_terms[0], ("dp", "seq"), scatter_dimension=0, tiled=True),
        lax.psum_scatter(grad_terms[1], ("dp", "seq"), scatter_dimension=0, tiled=True),
        lax.psum_scatter(grad_terms[2], ("dp", "seq"), scatter_dimension=0, tiled=True),
        lax.psum_scatter(grad_terms[3], ("dp", "seq"), scatter_dimension=0, tiled=True),
        lax.psum_scatter(grad_terms[4], ("dp", "seq"), scatter_dimension=0, tiled=True),
        lax.psum_scatter(grad_terms[5], ("dp", "seq"), scatter_dimension=0, tiled=True),
        lax.psum_scatter(grad_terms[6], ("dp", "seq"), scatter_dimension=0, tiled=True),
        lax.psum_scatter(grad_terms[7], ("dp", "seq"), scatter_dimension=0, tiled=True),
        lax.psum_scatter(grad_terms[8], ("dp", "seq"), scatter_dimension=0, tiled=True),
        lax.psum_scatter(grad_terms[9], ("dp", "seq"), scatter_dimension=0, tiled=True),
        lax.psum_scatter(grad_terms[10], ("dp", "seq"), scatter_dimension=0, tiled=True),
        lax.psum_scatter(grad_terms[11], ("dp", "seq"), scatter_dimension=0, tiled=True),
    )
    return (hidden_out, grad_in) + tuple(reduced)


def solution(mesh):
    return jax.shard_map(
        shards,
        mesh=mesh,
        in_specs=(
            P("dp", "seq", None),
            P("dp", None),
            P(),
            P(),
            P(),
            P(),
            P(),
            P(),
            P(),
            P(),
            P(),
            P(),
            P(),
            P(),
            P("dp", "seq", None),
        ),
        out_specs=(
            P("dp", "seq", None),
            P("dp", "seq", None),
            P(("dp", "seq")),
            P(("dp", "seq")),
            P(("dp", "seq")),
            P(("dp", "seq")),
            P(("dp", "seq"), None),
            P(("dp", "seq")),
            P(("dp", "seq"), None),
            P(("dp", "seq")),
            P(("dp", "seq"), None),
            P(("dp", "seq")),
            P(("dp", "seq"), None),
            P(("dp", "seq")),
        ),
        check_vma=False,
    )
```

profile of v0, /device:TPU:0, one launch (start us, length us, event | category | flops | bytes accessed | tf_op | source)
XLA Modules:
  0.0 1516.5 jit_solution(5117657675731257331)
XLA Ops:
  18.9 9.0 reduce.49
  31.7 6.9 all-to-all-start.2
  40.0 8.3 convolution_add_fusion
  48.3 6.6 copy.107
  61.1 27.4 %copy.139 = bf16[1,512,3072]{1,0,2:T(2,128)(2,1)} copy(bf16[1,512,3072]{1,2,0:T(8,128)(2,1)S(1)} %bitcast.395) | data formatting | bytes 6291456 | tf_op jit(solution)/shard_map/convert_element_type | solution.py:129
  88.6 22.0 %reduce.47 = bf16[3072,512]{1,0:T(8,128)(2,1)} reduce(bf16[3072,1,512]{2,1,0:T(2,128)(2,1)} %bitcast.392, bf16[]{:T(256)} %broadcast.808), dimensions={1}, to_apply=%bitcast.380.reduce_sub_computation | reduce | bytes 6291458
  136.2 55.2 %all-to-all-done = bf16[4,2,196608]{2,1,0:T(2,128)(2,1)} async-done(((bf16[4,2,196608]{2,1,0:T(2,128)(2,1)}), bf16[4,2,196608]{2,1,0:T(2,128)(2,1)}, u32[]{:S(2)}, u32[]{:S(2)}) %all-to-all-start) | async-done | bytes 3145760 | tf_op jit(solution)/shard_map/all_to_all | solution.py:132
  239.6 8.3 fusion.177
  248.0 8.1 fusion
  256.1 8.5 fusion.130
  294.6 7.6 multiply_convert_fusion.1
  315.2 12.7 fusion.181
  328.0 12.6 reduce.48
  348.4 11.5 multiply_reduce_fusion
  359.9 11.9 multiply_convert_fusion
  403.1 8.6 fusion.71
  414.2 15.7 %copy.125 = bf16[1,2048,768]{2,0,1:T(2,128)(2,1)} copy(bf16[1,2048,768]{1,2,0:T(8,128)(2,1)} %bitcast.397) | data formatting | bytes 6291456 | tf_op jit(solution)/shard_map/convert_element_type | solution.py:244
  429.9 33.3 %reduce.50 = bf16[2048,768]{1,0:T(8,128)(2,1)} reduce(bf16[2048,1,768]{2,1,0:T(2,128)(2,1)} %bitcast.391, bf16[]{:T(256)} %broadcast.808), dimensions={1}, to_apply=%bitcast.316.reduce_sub_computation | reduce | bytes 6291458
  467.7 118.8 %all_to_all.54 = bf16[4,2,196608]{2,1,0:T(2,128)(2,1)} all-to-all(bf16[4,2,196608]{2,1,0:T(2,128)(2,1)} %reshape.1434), channel_id=1, replica_groups=mesh['dp'=8,'seq'=4] {'seq'}, dimensions={0} | all-to-all | bytes 6291456 | tf_op jit(solution)/shard_map/all_to_all | solution.py:247
  599.2 6.5 copy.127
  614.6 6.9 fusion.136
  622.3 27.9 %multiply_convert_fusion.3 = (bf16[512,4096]{1,0:T(8,128)(2,1)}, f32[512,4096]{1,0:T(8,128)}, f32[512,4096]{1,0:T(8,128)}) fusion(f32[4096]{0:T(1024)S(1)} %copy-done.45, bf16[1024,4096]{1,0:T(8,128)(2,1)} %param.45, bf16[1,512,1024]{2,1,0:T(8,128)(2,1)S(1)} %copy-done.13, f32[1024]{0:T(1024)S(1)} %copy-done.49, f32[1024]{0:T(1024)S(1)} %copy-done.41, ...), kind=kOutput, calls=%fused_computation.25 | convolution fusion | flops 4436525056 | bytes 30437376 | tf_op jit(solution)/shard_map/dot_general | solution.py:169
  650.2 14.5 convert_reduce_fusion
  666.7 8.4 fusion.171
  675.4 13.4 fusion.164
  688.8 10.7 fusion.183
  699.5 7.3 fusion.182
  709.3 9.4 fusion.87
  721.4 41.4 %all-reduce.13 = (f32[1024]{0:T(1024)S(1)}, f32[1024]{0:T(1024)S(1)}, f32[1024]{0:T(1024)S(1)}, f32[1024]{0:T(1024)S(1)}, f32[3072]{0:T(1024)S(1)}, /*index=5*/f32[1024]{0:T(1024)S(1)}, f32[4096]{0:T(1024)S(1)}) all-reduce(f32[1024]{0:T(1024)S(1)} %get-tuple-element.128, ...), channel_id=2, replica_groups=mesh['dp'=8,'seq'=4] {'dp','seq'}, use_global_device_ids=true, to_apply=%region_23.24.clone | all-reduce | flops 12288 | bytes 98304
  766.3 11.3 reduce-scatter.5.cloned.1.call-done
  777.7 366.3 %reduce-scatter.9.cloned.1.call-done = f32[32,4096]{1,0:T(8,128)} async-done(((f32[1024,4096]{1,0:T(8,128)}), f32[32,4096]{1,0:T(8,128)}) %reduce-scatter.9.cloned.1.call-update) | async-done | bytes 524304 | tf_op jit(solution)/shard_map/reduce_scatter | solution.py:285
  1143.9 365.0 %reduce-scatter.11.cloned.1.call-done = f32[128,1024]{1,0:T(8,128)} async-done(((f32[4096,1024]{1,0:T(8,128)}), f32[128,1024]{1,0:T(8,128)}) %reduce-scatter.11.cloned.1.call-update) | async-done | bytes 524304 | tf_op jit(solution)/shard_map/reduce_scatter | solution.py:287
  (250 shorter events, 219.1 us)
Async XLA Ops:
  12.4 26.2 %copy-start.12 = (bf16[1,512,1024]{2,1,0:T(8,128)(2,1)S(1)}, bf16[1,512,1024]{2,1,0:T(8,128)(2,1)}, u32[]{:S(2)}) copy-start(bf16[1,512,1024]{2,1,0:T(8,128)(2,1)} %param.35) | copy-start | bytes 3145732
  18.9 21.1 %copy-start.42 = (f32[1024]{0:T(1024)S(1)}, f32[1024]{0:T(1024)}, u32[]{:S(2)}) copy-start(f32[1024]{0:T(1024)} %param.37) | copy-start | bytes 12292
  18.9 21.1 %copy-start.46 = (f32[3072]{0:T(1024)S(1)}, f32[3072]{0:T(1024)}, u32[]{:S(2)}) copy-start(f32[3072]{0:T(1024)} %param.42) | copy-start | bytes 36868
  18.9 21.1 %copy-start.47 = (f32[1024]{0:T(1024)S(1)}, f32[1024]{0:T(1024)}, u32[]{:S(2)}) copy-start(f32[1024]{0:T(1024)} %param.38) | copy-start | bytes 12292
  31.7 84.1 %all-to-all-start.2 = ((bf16[4,2,65536]{2,1,0:T(2,128)(2,1)}), bf16[4,2,65536]{2,1,0:T(2,128)(2,1)}, u32[]{:S(2)}, u32[]{:S(2)}) async-start(bf16[4,2,65536]{2,1,0:T(2,128)(2,1)} %reshape.1432), calls=%async_computation.2 | async-start | bytes 2097152 | tf_op jit(solution)/shard_map/all_to_all | solution.py:185
  115.8 75.6 %all-to-all-start = ((bf16[4,2,196608]{2,1,0:T(2,128)(2,1)}), bf16[4,2,196608]{2,1,0:T(2,128)(2,1)}, u32[]{:S(2)}, u32[]{:S(2)}) async-start(bf16[4,2,196608]{2,1,0:T(2,128)(2,1)} %reshape.1428), calls=%async_computation | async-start | bytes 6291456 | tf_op jit(solution)/shard_map/all_to_all | solution.py:132
  213.9 11.3 copy-start.14
  213.9 13.4 copy-start.16
  213.9 13.4 copy-start.19
  266.5 10.7 slice-start.3
  266.5 7.5 copy-start.23
  266.5 10.7 slice-start.4
  271.3 10.2 copy-start.10
  294.6 9.7 slice-start.5
  294.6 7.6 copy-start.17
  294.6 9.6 slice-start.6
  344.1 44.0 %all-to-all-start.1 = ((bf16[4,2,65536]{2,1,0:T(2,128)(2,1)}), bf16[4,2,65536]{2,1,0:T(2,128)(2,1)}, u32[]{:S(2)}, u32[]{:S(2)}) async-start(bf16[4,2,65536]{2,1,0:T(2,128)(2,1)} %reshape.1430), calls=%async_computation.1 | async-start | bytes 2097152 | tf_op jit(solution)/shard_map/all_to_all | solution.py:163
  348.3 418.0 %reduce-scatter.7.cloned.1.call-start = ((), (), s32[]{:S(2)}) async-start(), calls=%async_computation.9 | async-start | bytes 4325376 | tf_op jit(solution)/shard_map/reduce_scatter | solution.py:283
  359.9 16.7 %copy-start.18 = (bf16[1,2048,4,64]{1,3,2,0:T(8,128)(2,1)S(1)}, bf16[1,2048,4,64]{1,3,2,0:T(8,128)(2,1)}, u32[]{:S(2)}) copy-start(bf16[1,2048,4,64]{1,3,2,0:T(8,128)(2,1)} %copy-done.16) | copy-start | bytes 3145732
  371.8 11.8 slice-start
  388.0 9.0 copy-start.38
  401.9 375.8 %reduce-scatter.5.cloned.1.call-start = ((), (), s32[]{:S(2)}) async-start(), calls=%async_computation.8 | async-start | bytes 12976128 | tf_op jit(solution)/shard_map/reduce_scatter | solution.py:281
  403.1 8.6 copy-start.21
  599.2 8.3 copy-start.44
  621.6 522.4 %reduce-scatter.9.cloned.1.call-start = ((), (), s32[]{:S(2)}) async-start(), calls=%async_computation.10 | async-start | bytes 17301504 | tf_op jit(solution)/shard_map/reduce_scatter | solution.py:285
  622.3 27.9 %copy-start.27 = (bf16[1,512,1024]{2,1,0:T(8,128)(2,1)S(1)}, bf16[1,512,1024]{2,1,0:T(8,128)(2,1)}, u32[]{:S(2)}) copy-start(bf16[1,512,1024]{2,1,0:T(8,128)(2,1)} %param.49) | copy-start | bytes 3145732
  675.1 833.8 %reduce-scatter.11.cloned.1.call-start = ((), (), s32[]{:S(2)}) async-start(), calls=%async_computation.11 | async-start | bytes 17301504 | tf_op jit(solution)/shard_map/reduce_scatter | solution.py:287
  688.8 10.7 copy-start.54
  699.5 7.4 copy-start.51
  709.3 9.4 copy-start.24
  709.3 9.4 copy-start.28
  763.4 746.1 %copy-start.53 = (f32[32]{0:T(128)}, f32[32]{0:T(128)S(1)}, u32[]{:S(2)}) copy-start(f32[32]{0:T(128)S(1)} %dynamic-slice.67) | copy-start | bytes 388
  (38 other events, 113.4 us)
Sparse Core Ops, SparseCore 0:
  402.0 176.7 reduce-scatter.6
  621.7 155.9 reduce-scatter.4
  780.6 363.2 reduce-scatter.8
  1146.8 362.1 reduce-scatter.10
where the time goes:
time: 1530 us; the launch traced here: 1520 us
  waiting for transfers between devices  798 us (52%)
  matrix products  210 us (14%)
  local copies, waits for them, and re-layouts  160 us (10%)
  blocking collectives  160 us (10%)
  other arithmetic  156 us (10%)
  starting transfers between devices  16.8 us (1%)
    reduce_scatter x1, waiting for transfers between devices, shards(): lax.psum_scatter(grad_terms[8], ('dp', 'seq'), scatter_dimension=0, tiled...  366 us
    reduce_scatter x1, waiting for transfers between devices, shards(): lax.psum_scatter(grad_terms[10], ('dp', 'seq'), scatter_dimension=0, tile...  365 us
    all_to_all x1, blocking collectives, shards(): lax.all_to_all(d_heads, 'seq', split_axis=1, concat_axis=2, tiled=True)  119 us
    unnamed x8, other arithmetic  89.7 us
    unnamed x146, local copies, waits for them, and re-layouts  61.3 us
    all_to_all x1, waiting for transfers between devices, shards(): lax.all_to_all(turned, 'seq', split_axis=2, concat_axis=1, tiled=True)  55.2 us
    unnamed x1, blocking collectives  41.4 us
    dot_general x4, matrix products, transpose_dot(): lax.dot_general(left, right, (((0,), (0,)), ((), ())), preferred_element_...  33.6 us
  transfers between devices with their start and end apart: 7, of which 4 were waited for; matrix products, arithmetic and copies ran while one was open for 22% of the time, Pallas kernels for 0%

commit v1 on v0

--- a/solution.py
+++ b/solution.py
@@ -8,6 +8,13 @@
 ROT = 16
 epsilon = 1e-05
 masked_score = -1e30
+
+
+def swap_blocks(block, mesh_axis, split, join):
+    size = lax.axis_size(mesh_axis)
+    tiles = jnp.stack(jnp.split(block, size, axis=split), axis=0)
+    tiles = lax.all_to_all(tiles, mesh_axis, split_axis=0, concat_axis=0)
+    return jnp.concatenate(tiles, axis=join)
 
 
 def layout(lengths, positions):
@@ -244,9 +251,7 @@
         .astype(jnp.bfloat16)
         .reshape(seqs_here, full_len, heads_here * 3 * HEAD)
     )
-    d_tokens = lax.all_to_all(d_heads, "seq", split_axis=1, concat_axis=2, tiled=True).reshape(
-        row_count, HEADS, 3, HEAD
-    )
+    d_tokens = swap_blocks(d_heads, "seq", 1, 2).reshape(row_count, HEADS, 3, HEAD)
     _, rotate_pull = jax.vjp(lambda packed: rotate(packed, cosine, sine_part), shaped)
     d_qkv = (
         rotate_pull(d_tokens.astype(jnp.float32))[0]

time: 1530 us -> 1490 us (0.974)
  local copies, waits for them, and re-layouts: 160 us -> 121 us
  other arithmetic: 156 us -> 119 us
  blocking collectives: 160 us -> 182 us
  waiting for transfers between devices: 798 us -> 818 us
    unnamed x8 -> x6, other arithmetic: 89.7 us -> 56.4 us
    convert_element_type x2 -> x0, local copies, waits for them, and re-layouts: 22.3 us -> none  [the longest x1 15.7 us: shards(): d_heads = jnp.stack([d_queries, d_keys, d_values], axis=3).astype(jnp.bfl...]
    all_to_all x1, blocking collectives: 119 us -> 141 us  [swap_blocks(): tiles = lax.all_to_all(tiles, mesh_axis, split_axis=0, concat_axis=0)]
    reduce_scatter x1, waiting for transfers between devices: 11.3 us -> 31.4 us  [shards(): lax.psum_scatter(grad_terms[4], ('dp', 'seq'), scatter_dimension=0, tiled...]
    unnamed x146 -> x142, local copies, waits for them, and re-layouts: 61.3 us -> 52.8 us
  transfers between devices with their start and end apart: 7 -> 7, of which waited for: 4 -> 4; matrix products, arithmetic and copies ran while one was open for 22% -> 17% of each run, Pallas kernels for 0% -> 0%
where the time goes in v1:
time: 1490 us; the launch traced here: 1480 us
  waiting for transfers between devices  818 us (55%)
  matrix products  211 us (14%)
  blocking collectives  182 us (12%)
  local copies, waits for them, and re-layouts  121 us (8%)
  other arithmetic  119 us (8%)
  starting transfers between devices  16.8 us (1%)
  between operations  15.1 us (1%)
    reduce_scatter x1, waiting for transfers between devices, shards(): lax.psum_scatter(grad_terms[8], ('dp', 'seq'), scatter_dimension=0, tiled...  366 us
    reduce_scatter x1, waiting for transfers between devices, shards(): lax.psum_scatter(grad_terms[10], ('dp', 'seq'), scatter_dimension=0, tile...  365 us
    all_to_all x1, blocking collectives, swap_blocks(): tiles = lax.all_to_all(tiles, mesh_axis, split_axis=0, concat_axis=0)  141 us
    unnamed x6, other arithmetic  56.4 us
    all_to_all x1, waiting for transfers between devices, shards(): lax.all_to_all(turned, 'seq', split_axis=2, concat_axis=1, tiled=True)  55.2 us
    unnamed x142, local copies, waits for them, and re-layouts  52.8 us
    unnamed x1, blocking collectives  41.5 us
    dot_general x4, matrix products, transpose_dot(): lax.dot_general(left, right, (((0,), (0,)), ((), ())), preferred_element_...  34.2 us
  transfers between devices with their start and end apart: 7, of which 4 were waited for; matrix products, arithmetic and copies ran while one was open for 17% of the time, Pallas kernels for 0%

profile of v1, /device:TPU:0, one launch (start us, length us, event | category | flops | bytes accessed | tf_op | source)
XLA Modules:
  0.0 1483.5 jit_solution(2382249987254178397)
XLA Ops:
  15.8 9.0 reduce.49
  28.6 6.9 all-to-all-start.2
  36.8 8.3 convolution_add_fusion
  45.1 6.6 copy.108
  57.9 27.4 %copy.140 = bf16[1,512,3072]{1,0,2:T(2,128)(2,1)} copy(bf16[1,512,3072]{1,2,0:T(8,128)(2,1)S(1)} %bitcast.396) | data formatting | bytes 6291456 | tf_op jit(solution)/shard_map/convert_element_type | solution.py:136
  85.4 22.0 %reduce.47 = bf16[3072,512]{1,0:T(8,128)(2,1)} reduce(bf16[3072,1,512]{2,1,0:T(2,128)(2,1)} %bitcast.393, bf16[]{:T(256)} %broadcast.808), dimensions={1}, to_apply=%bitcast.384.reduce_sub_computation | reduce | bytes 6291458
  133.0 55.2 %all-to-all-done = bf16[4,2,196608]{2,1,0:T(2,128)(2,1)} async-done(((bf16[4,2,196608]{2,1,0:T(2,128)(2,1)}), bf16[4,2,196608]{2,1,0:T(2,128)(2,1)}, u32[]{:S(2)}, u32[]{:S(2)}) %all-to-all-start) | async-done | bytes 3145760 | tf_op jit(solution)/shard_map/all_to_all | solution.py:139
  202.2 6.3 reshape.1396
  237.8 8.3 fusion.177
  246.1 8.1 fusion
  254.2 8.5 fusion.130
  284.3 7.0 multiply_convert_fusion.2
  298.1 6.3 multiply_reduce_fusion.1
  304.4 6.4 multiply_convert_fusion.1
  318.9 12.7 fusion.181
  331.7 12.6 reduce.48
  352.0 11.7 multiply_reduce_fusion
  363.8 11.9 multiply_convert_fusion
  404.4 8.2 fusion.71
  414.1 140.6 %all_to_all.50 = bf16[4,1,512,768]{2,3,1,0:T(8,128)(2,1)S(1)} all-to-all(bf16[4,1,512,768]{2,3,1,0:T(8,128)(2,1)S(1)} %pad_maximum_fusion.1), channel_id=1, replica_groups=mesh['dp'=8,'seq'=4] {'seq'}, dimensions={0} | all-to-all | bytes 6291456 | tf_op jit(solution)/shard_map/all_to_all | solution.py:16
  561.1 6.9 fusion.136
  568.7 27.9 %multiply_convert_fusion.3 = (bf16[512,4096]{1,0:T(8,128)(2,1)}, f32[512,4096]{1,0:T(8,128)}, f32[512,4096]{1,0:T(8,128)}) fusion(f32[4096]{0:T(1024)S(1)} %copy-done.46, bf16[1024,4096]{1,0:T(8,128)(2,1)} %param.45, bf16[1,512,1024]{2,1,0:T(8,128)(2,1)S(1)} %copy-done.13, f32[1024]{0:T(1024)S(1)} %copy-done.50, f32[1024]{0:T(1024)S(1)} %copy-done.42, ...), kind=kOutput, calls=%fused_computation.25 | convolution fusion | flops 4436525056 | bytes 30437376 | tf_op jit(solution)/shard_map/dot_general | solution.py:176
  596.7 14.5 convert_reduce_fusion
  613.1 8.9 fusion.171
  622.4 13.6 fusion.164
  636.0 10.6 fusion.183
  646.6 7.3 fusion.182
  656.3 9.1 fusion.87
  668.1 41.5 %all-reduce.13 = (f32[1024]{0:T(1024)S(1)}, f32[1024]{0:T(1024)S(1)}, f32[1024]{0:T(1024)S(1)}, f32[1024]{0:T(1024)S(1)}, f32[3072]{0:T(1024)S(1)}, /*index=5*/f32[1024]{0:T(1024)S(1)}, f32[4096]{0:T(1024)S(1)}) all-reduce(f32[1024]{0:T(1024)S(1)} %get-tuple-element.128, ...), channel_id=2, replica_groups=mesh['dp'=8,'seq'=4] {'dp','seq'}, use_global_device_ids=true, to_apply=%region_23.24.clone | all-reduce | flops 12288 | bytes 98304
  713.1 31.4 %reduce-scatter.5.cloned.1.call-done = f32[32,3072]{1,0:T(8,128)} async-done(((f32[1024,3072]{1,0:T(8,128)}), f32[32,3072]{1,0:T(8,128)}) %reduce-scatter.5.cloned.1.call-update) | async-done | bytes 393232 | tf_op jit(solution)/shard_map/reduce_scatter | solution.py:286
  744.6 366.4 %reduce-scatter.9.cloned.1.call-done = f32[32,4096]{1,0:T(8,128)} async-done(((f32[1024,4096]{1,0:T(8,128)}), f32[32,4096]{1,0:T(8,128)}) %reduce-scatter.9.cloned.1.call-update) | async-done | bytes 524304 | tf_op jit(solution)/shard_map/reduce_scatter | solution.py:290
  1110.9 365.0 %reduce-scatter.11.cloned.1.call-done = f32[128,1024]{1,0:T(8,128)} async-done(((f32[4096,1024]{1,0:T(8,128)}), f32[128,1024]{1,0:T(8,128)}) %reduce-scatter.11.cloned.1.call-update) | async-done | bytes 524304 | tf_op jit(solution)/shard_map/reduce_scatter | solution.py:292
  (243 shorter events, 181.1 us)
Async XLA Ops:
  15.3 20.2 %copy-start.12 = (bf16[1,512,1024]{2,1,0:T(8,128)(2,1)S(1)}, bf16[1,512,1024]{2,1,0:T(8,128)(2,1)}, u32[]{:S(2)}) copy-start(bf16[1,512,1024]{2,1,0:T(8,128)(2,1)} %param.35) | copy-start | bytes 3145732
  15.8 21.0 %copy-start.43 = (f32[1024]{0:T(1024)S(1)}, f32[1024]{0:T(1024)}, u32[]{:S(2)}) copy-start(f32[1024]{0:T(1024)} %param.37) | copy-start | bytes 12292
  15.8 21.0 %copy-start.47 = (f32[3072]{0:T(1024)S(1)}, f32[3072]{0:T(1024)}, u32[]{:S(2)}) copy-start(f32[3072]{0:T(1024)} %param.42) | copy-start | bytes 36868
  15.8 21.0 %copy-start.48 = (f32[1024]{0:T(1024)S(1)}, f32[1024]{0:T(1024)}, u32[]{:S(2)}) copy-start(f32[1024]{0:T(1024)} %param.38) | copy-start | bytes 12292
  28.6 84.0 %all-to-all-start.2 = ((bf16[4,2,65536]{2,1,0:T(2,128)(2,1)}), bf16[4,2,65536]{2,1,0:T(2,128)(2,1)}, u32[]{:S(2)}, u32[]{:S(2)}) async-start(bf16[4,2,65536]{2,1,0:T(2,128)(2,1)} %reshape.1428), calls=%async_computation.2 | async-start | bytes 2097152 | tf_op jit(solution)/shard_map/all_to_all | solution.py:192
  112.6 75.6 %all-to-all-start = ((bf16[4,2,196608]{2,1,0:T(2,128)(2,1)}), bf16[4,2,196608]{2,1,0:T(2,128)(2,1)}, u32[]{:S(2)}, u32[]{:S(2)}) async-start(bf16[4,2,196608]{2,1,0:T(2,128)(2,1)} %reshape.1424), calls=%async_computation | async-start | bytes 6291456 | tf_op jit(solution)/shard_map/all_to_all | solution.py:139
  210.7 11.3 copy-start.14
  210.7 14.8 copy-start.16
  210.8 14.8 copy-start.19
  264.6 10.7 slice-start.3
  264.6 7.5 copy-start.23
  264.7 10.7 slice-start.4
  269.5 10.2 copy-start.10
  347.7 42.7 %all-to-all-start.1 = ((bf16[4,2,65536]{2,1,0:T(2,128)(2,1)}), bf16[4,2,65536]{2,1,0:T(2,128)(2,1)}, u32[]{:S(2)}, u32[]{:S(2)}) async-start(bf16[4,2,65536]{2,1,0:T(2,128)(2,1)} %reshape.1426), calls=%async_computation.1 | async-start | bytes 2097152 | tf_op jit(solution)/shard_map/all_to_all | solution.py:170
  352.0 361.1 %reduce-scatter.7.cloned.1.call-start = ((), (), s32[]{:S(2)}) async-start(), calls=%async_computation.9 | async-start | bytes 4325376 | tf_op jit(solution)/shard_map/reduce_scatter | solution.py:288
  363.8 16.0 %copy-start.11 = (bf16[4,512,512]{1,2,0:T(8,128)(2,1)S(1)}, bf16[4,512,512]{1,2,0:T(8,128)(2,1)}, u32[]{:S(2)}) copy-start(bf16[4,512,512]{1,2,0:T(8,128)(2,1)} %copy-done.10) | copy-start | bytes 6291460
  375.7 10.4 slice-start
  375.7 10.4 slice-start.1
  390.5 9.0 copy-start.39
  404.3 340.3 %reduce-scatter.5.cloned.1.call-start = ((), (), s32[]{:S(2)}) async-start(), calls=%async_computation.8 | async-start | bytes 12976128 | tf_op jit(solution)/shard_map/reduce_scatter | solution.py:286
  404.3 8.2 copy-start.20
  404.4 8.2 copy-start.21
  568.0 542.9 %reduce-scatter.9.cloned.1.call-start = ((), (), s32[]{:S(2)}) async-start(), calls=%async_computation.10 | async-start | bytes 17301504 | tf_op jit(solution)/shard_map/reduce_scatter | solution.py:290
  568.7 27.9 %copy-start.28 = (bf16[1,512,1024]{2,1,0:T(8,128)(2,1)S(1)}, bf16[1,512,1024]{2,1,0:T(8,128)(2,1)}, u32[]{:S(2)}) copy-start(bf16[1,512,1024]{2,1,0:T(8,128)(2,1)} %param.49) | copy-start | bytes 3145732
  622.1 853.9 %reduce-scatter.11.cloned.1.call-start = ((), (), s32[]{:S(2)}) async-start(), calls=%async_computation.11 | async-start | bytes 17301504 | tf_op jit(solution)/shard_map/reduce_scatter | solution.py:292
  635.9 10.6 copy-start.55
  646.6 7.3 copy-start.25
  646.6 7.3 copy-start.51
  646.6 7.3 copy-start.52
  656.3 9.2 copy-start.24
  656.3 9.2 copy-start.29
  710.2 766.3 %copy-start.54 = (f32[32]{0:T(128)}, f32[32]{0:T(128)S(1)}, u32[]{:S(2)}) copy-start(f32[32]{0:T(128)S(1)} %dynamic-slice.67) | copy-start | bytes 388
  (37 other events, 92.7 us)
Sparse Core Ops, SparseCore 0:
  404.4 178.2 reduce-scatter.6
  589.3 155.2 reduce-scatter.4
  747.6 363.3 reduce-scatter.8
  1113.8 362.1 reduce-scatter.10
